TPU v7x, 128 devices: a whole 4x4x4 slice. The times are simulated.
128 devices in a mesh: dp: 8 (over x, y_lo), tensor: 16 (over y_hi, z, core).
Axes of the slice: x: 4, y: 4 (y_hi: 2, y_lo: 2; y = y_hi * 2 + y_lo), z: 4, core: 2. Of those that a mesh axis runs over, the one named last changes fastest.
Arguments:
- enc_tokens: bfloat16 [128, 128, 1024], P(('dp', 'tensor')), may hold values from -6 to 6
- src_lengths: int32 [128], replicated, may hold values from 1 to 128, as said below
- enc_gain: float32 [1024], replicated, may hold values from 0.1 to 1.9
- enc_query: bfloat16 [1024, 8192], P(None, 'tensor'), may hold values from -0.1875 to 0.1875
- enc_key: bfloat16 [1024, 8192], P(None, 'tensor'), may hold values from -0.1875 to 0.1875
- enc_value: bfloat16 [1024, 8192], P(None, 'tensor'), may hold values from -0.1875 to 0.1875
- enc_output: bfloat16 [8192, 1024], P('tensor'), may hold values from -0.0625 to 0.0625
- enc_bias: float32 [64, 33], P('tensor'), may hold values from -3 to 260
- mem_gain: float32 [1024], replicated, may hold values from 0.1 to 1.9
- dec_tokens: bfloat16 [128, 64, 1024], P(('dp', 'tensor')), may hold values from -6 to 6
- tgt_lengths: int32 [128], P(('dp', 'tensor')), may hold values from 1 to 64
- lang_tags: int32 [128], P('dp'), may hold values from 0 to 7
- lang_table: bfloat16 [8, 1024], replicated, may hold values from -6 to 6
- cross_gain: float32 [1024], replicated, may hold values from 0.1 to 1.9
- cross_query: bfloat16 [1024, 8192], P(None, 'tensor'), may hold values from -0.1875 to 0.1875
- cross_key: bfloat16 [1024, 8192], P(None, 'tensor'), may hold values from -0.1875 to 0.1875
- cross_value: bfloat16 [1024, 8192], P(None, 'tensor'), may hold values from -0.1875 to 0.1875
- cross_output: bfloat16 [8192, 1024], P('tensor'), may hold values from -0.0625 to 0.0625
- ffn_gain: float32 [1024], replicated, may hold values from 0.1 to 1.9
- ffn_in: bfloat16 [1024, 32768], P(None, 'tensor'), may hold values from -0.1875 to 0.1875
- ffn_out: bfloat16 [32768, 1024], P('tensor'), may hold values from -0.03125 to 0.03125
Outputs:
- enc_memory: bfloat16 [128, 128, 1024], P(('dp', 'tensor'))
- dec_out: bfloat16 [128, 64, 1024], P(('dp', 'tensor'))
Inputs may be any that keep to these rules, and one draw needn't show every extreme that they name: `src_lengths`: never falling along the batch; the first is 1 and the last is 128.
All inputs are finite; a program needn't handle non-finite values.
Results may differ from a plain program's by a relative error of at most 0.014.
Values may be sent and summed in bfloat16 or wider, within the bound.
A program may use at most 128 MiB of HBM per device.

v0:
```python
import jax
import jax.numpy as jnp
from jax import lax
from jax.sharding import PartitionSpec as P

HD = 128
MAXREL = 16
NB = 33
EPSILON = 1e-06
NEG_FILL = -1e30


def rms_norm(values, norm_gain):
    mean_sq = jnp.mean(values * values, axis=-1, keepdims=True)
    return values * lax.rsqrt(mean_sq + EPSILON) * norm_gain


def make_grid(bias_table, query_len, key_len):
    offset = jnp.arange(key_len)[None, :] - jnp.arange(query_len)[:, None]
    bucket = (jnp.clip(offset, -MAXREL, MAXREL) + MAXREL).reshape(1, query_len * key_len)
    onehot = (bucket == jnp.arange(NB)[:, None]).astype(jnp.float32)
    flat_grid = jnp.dot(
        bias_table, onehot, precision=lax.Precision.HIGHEST, preferred_element_type=jnp.float32
    )
    return flat_grid.reshape(bias_table.shape[0], query_len, key_len)


def attend(query_rows, key_rows, value_rows, bias_table, lengths):
    examples, query_len, columns = query_rows.shape
    key_len = key_rows.shape[1]
    head_count = columns // HD
    query_heads = query_rows.reshape(examples, query_len, head_count, HD)
    key_heads = key_rows.reshape(examples, key_len, head_count, HD)
    value_heads = value_rows.reshape(examples, key_len, head_count, HD)
    scores = jnp.einsum(
        "eqhd,ekhd->ehqk", query_heads, key_heads, preferred_element_type=jnp.float32
    )
    scores = scores * HD ** (-0.5)
    if bias_table is not None:
        scores = scores + make_grid(bias_table, query_len, key_len)[None]
    key_valid = jnp.arange(key_len)[None, :] < lengths[:, None]
    scores = jnp.where(key_valid[:, None, None, :], scores, NEG_FILL)
    row_max = jnp.max(scores, axis=-1, keepdims=True)
    exponent = jnp.exp(scores - row_max)
    weights = (exponent / jnp.sum(exponent, axis=-1, keepdims=True)).astype(jnp.bfloat16)
    context = jnp.einsum(
        "ehqk,ekhd->eqhd", weights, value_heads, preferred_element_type=jnp.float32
    )
    return context.astype(jnp.bfloat16).reshape(examples, query_len, columns)


def widen(values):
    return lax.all_gather(values, "tensor", axis=0, tiled=True)


def narrow(partial_value):
    return lax.psum_scatter(
        partial_value.astype(jnp.bfloat16), "tensor", scatter_dimension=0, tiled=True
    ).astype(jnp.float32)


def restripe(values):
    groups = lax.axis_size("dp")
    per_pair = values.shape[0] // groups
    shaped = values.reshape((per_pair, groups) + values.shape[1:])
    arrived = lax.all_to_all(shaped, "dp", split_axis=1, concat_axis=0, tiled=True)
    return arrived.reshape(values.shape)


def project(rows, weight):
    flat_rows = rows.reshape(-1, rows.shape[-1])
    result = jnp.dot(flat_rows, weight, preferred_element_type=jnp.float32).astype(jnp.bfloat16)
    return result.reshape(rows.shape[:-1] + (weight.shape[1],))


def output_terms(context, weight):
    flat_rows = context.reshape(-1, context.shape[-1])
    result = jnp.dot(flat_rows, weight, preferred_element_type=jnp.float32)
    return result.reshape(context.shape[:-1] + (weight.shape[1],))


def on_device(
    enc_tokens,
    src_lengths,
    enc_gain,
    enc_query,
    enc_key,
    enc_value,
    enc_output,
    enc_bias,
    mem_gain,
    dec_tokens,
    tgt_lengths,
    lang_tags,
    lang_table,
    cross_gain,
    cross_query,
    cross_key,
    cross_value,
    cross_output,
    ffn_gain,
    ffn_in,
    ffn_out,
):
    groups = lax.axis_size("dp")
    group_index = lax.axis_index("dp")
    tensor_index = lax.axis_index("tensor")
    local_ex = enc_tokens.shape[0]
    examples = local_ex * lax.axis_size("tensor")
    per_pair = examples // groups
    enc_len = lax.dynamic_slice_in_dim(src_lengths, group_index * examples, examples)
    dec_src_len = lax.dynamic_index_in_dim(
        src_lengths.reshape(groups, per_pair, groups), group_index, axis=2, keepdims=False
    ).reshape(examples)
    enc_input = enc_tokens.astype(jnp.float32)
    enc_normed = rms_norm(enc_input, enc_gain).astype(jnp.bfloat16)
    enc_rows = widen(enc_normed)
    enc_context = attend(
        project(enc_rows, enc_query),
        project(enc_rows, enc_key),
        project(enc_rows, enc_value),
        enc_bias,
        enc_len,
    )
    enc_hidden = enc_input + narrow(output_terms(enc_context, enc_output))
    enc_memory = rms_norm(enc_hidden, mem_gain).astype(jnp.bfloat16)
    dec_memory = restripe(widen(enc_memory))
    cross_k = project(dec_memory, cross_key)
    cross_v = project(dec_memory, cross_value)
    lang_onehot = (lang_tags[:, None] == jnp.arange(lang_table.shape[0])[None, :]).astype(
        jnp.bfloat16
    )
    lang_rows = jnp.dot(lang_onehot, lang_table, preferred_element_type=jnp.float32)[:, None, :]
    dec_full = widen(dec_tokens).astype(jnp.float32) + lang_rows
    dec_normed = rms_norm(dec_full, cross_gain).astype(jnp.bfloat16)
    cross_context = attend(project(dec_normed, cross_query), cross_k, cross_v, None, dec_src_len)
    cross_terms = output_terms(cross_context, cross_output)
    local_lang = lax.dynamic_slice_in_dim(lang_rows, tensor_index * local_ex, local_ex, 0)
    hidden_local = dec_tokens.astype(jnp.float32) + local_lang + narrow(cross_terms)
    ffn_rows = widen(rms_norm(hidden_local, ffn_gain).astype(jnp.bfloat16))
    flat_rows = ffn_rows.reshape(-1, ffn_rows.shape[-1])
    activated = jnp.maximum(
        jnp.dot(flat_rows, ffn_in, preferred_element_type=jnp.float32), 0.0
    ).astype(jnp.bfloat16)
    activated = activated.reshape(ffn_rows.shape[:-1] + (ffn_in.shape[1],))
    dec_sum = hidden_local + narrow(output_terms(activated, ffn_out))
    target_len = dec_tokens.shape[1]
    keep = jnp.arange(target_len)[None, :] < tgt_lengths[:, None]
    dec_out = jnp.where(keep[:, :, None], dec_sum, 0.0).astype(jnp.bfloat16)
    return (enc_memory, dec_out)


def solution(mesh):
    in_specs = (
        P(("dp", "tensor"), None, None),
        P(),
        P(),
        P(None, "tensor"),
        P(None, "tensor"),
        P(None, "tensor"),
        P("tensor", None),
        P("tensor", None),
        P(),
        P(("dp", "tensor"), None, None),
        P(("dp", "tensor")),
        P("dp"),
        P(),
        P(),
        P(None, "tensor"),
        P(None, "tensor"),
        P(None, "tensor"),
        P("tensor", None),
        P(),
        P(None, "tensor"),
        P("tensor", None),
    )
    out_specs = (P(("dp", "tensor"), None, None), P(("dp", "tensor"), None, None))
    return jax.shard_map(
        on_device, mesh=mesh, in_specs=in_specs, out_specs=out_specs, check_vma=False
    )
```

profile of v0, /device:TPU:0, one launch (start us, length us, event | category | flops | bytes accessed | tf_op | source)
XLA Modules:
  0.0 565.8 jit_solution(7086477349250466452)
XLA Ops:
  7.2 0.0 all-gather.5.cloned.1.call-start
  7.2 1.2 fusion.39
  8.5 1.8 fusion.41
  10.3 0.0 all-gather.5.cloned.1.call-update
  10.3 0.0 reduce-scatter.4.cloned.1.call-start
  10.4 1.7 fusion.29
  12.1 0.1 copy.66
  12.2 0.1 dynamic_slice.8
  12.3 0.1 iota_compare_fusion.6
  12.4 56.7 %all-gather.5.cloned.1.call-done = bf16[16,128,1024]{2,1,0:T(8,128)(2,1)} async-done(((bf16[1,128,1024]{2,1,0:T(8,128)(2,1)}), bf16[16,128,1024]{2,1,0:T(8,128)(2,1)}) %all-gather.5.cloned.1.call-update) | async-done | bytes 4194320 | tf_op jit(solution)/shard_map/all_gather | solution.py:53
  69.0 5.9 %convolution_convert_fusion.2 = bf16[2048,512]{1,0:T(8,128)(2,1)} fusion(bf16[2048,1024]{1,0:T(8,128)(2,1)} %bitcast.61, bf16[1024,512]{1,0:T(8,128)(2,1)S(1)} %copy-done.16), kind=kOutput, calls=%fused_computation.11 | convolution fusion | flops 2148532224 | bytes 7340032 | tf_op jit(solution)/shard_map/dot_general | solution.py:72
  74.9 2.5 reshape_reshape.26
  77.5 6.3 %convolution_convert_fusion.3 = bf16[2048,512]{1,0:T(8,128)(2,1)} fusion(bf16[2048,1024]{1,0:T(8,128)(2,1)} %bitcast.62, bf16[1024,512]{1,0:T(8,128)(2,1)} %param.24), kind=kOutput, calls=%fused_computation.12 | convolution fusion | flops 2148532224 | bytes 7340032 | tf_op jit(solution)/shard_map/dot_general | solution.py:72
  83.8 3.7 convolution_convert_fusion.4
  87.5 4.0 reshape_reshape.24
  91.4 4.0 reshape_reshape.25
  95.4 3.2 fusion.10
  98.6 1.8 fusion.54
  100.4 0.9 fusion.18
  101.3 4.3 convolution_convert_fusion.5
  105.7 0.0 all-gather.7.cloned.1.call-start
  105.7 78.5 %reduce-scatter.4.cloned.1.call-done = bf16[1,128,1024]{2,1,0:T(8,128)(2,1)} async-done(((bf16[16,128,1024]{2,1,0:T(8,128)(2,1)}), bf16[1,128,1024]{2,1,0:T(8,128)(2,1)}) %reduce-scatter.4.cloned.1.call-update) | async-done | bytes 262160 | tf_op jit(solution)/shard_map/reduce_scatter | solution.py:57
  184.2 1.1 multiply_reduce_fusion.1
  185.4 1.8 multiply_convert_fusion.1
  187.1 0.0 all-gather.7.cloned.1.call-update
  187.2 0.0 all-gather.9.cloned.1.call-start
  187.2 0.5 all-gather.9.cloned.1.call-update
  187.7 54.1 %all-gather.7.cloned.1.call-done = bf16[16,128,1024]{2,1,0:T(8,128)(2,1)} async-done(((bf16[1,128,1024]{2,1,0:T(8,128)(2,1)}), bf16[16,128,1024]{2,1,0:T(8,128)(2,1)}) %all-gather.7.cloned.1.call-update) | async-done | bytes 4194320 | tf_op jit(solution)/shard_map/all_gather | solution.py:53
  241.8 4.8 copy.70
  246.6 4.7 all-to-all-start
  251.3 0.3 reduce-scatter.6.cloned.1.call-start
  251.6 0.1 reshape.171
  251.7 0.3 dynamic-slice_reduce_fusion
  252.0 0.1 lt.72
  252.0 0.1 iota_compare_fusion.4
  252.1 0.2 fusion.42
  252.3 60.9 %all-gather.9.cloned.1.call-done = bf16[16,64,1024]{2,1,0:T(8,128)(2,1)} async-done(((bf16[1,64,1024]{2,1,0:T(8,128)(2,1)}), bf16[16,64,1024]{2,1,0:T(8,128)(2,1)}) %all-gather.9.cloned.1.call-update) | async-done | bytes 2097168 | tf_op jit(solution)/shard_map/all_gather | solution.py:53
  313.2 2.4 multiply_reduce_fusion
  315.6 0.7 multiply_convert_fusion
  316.3 0.5 copy-done.18
  316.8 1.2 convolution_convert_fusion.8
  318.1 0.3 reshape_reshape.29
  318.4 0.9 copy-done.19
  319.3 5.9 %convolution_convert_fusion = bf16[2048,512]{1,0:T(8,128)(2,1)} fusion(bf16[2048,1024]{1,0:T(8,128)(2,1)} %bitcast.11, bf16[1024,512]{1,0:T(8,128)(2,1)S(1)} %copy-done.19), kind=kOutput, calls=%fused_computation.9 | convolution fusion | flops 2148532224 | bytes 7340032 | tf_op jit(solution)/shard_map/dot_general | solution.py:72
  325.3 4.5 convolution_convert_fusion.1
  329.8 2.1 reshape_reshape.28
  331.9 2.5 reshape_reshape.30
  334.4 1.5 fusion.7
  336.0 1.3 copy-done.7
  337.3 1.2 fusion.55
  338.5 0.4 copy-done.6
  338.9 9.8 %fusion.25 = bf16[16,4,8,8,128]{4,3,2,1,0:T(8,128)(2,1)} fusion(bf16[16,128,4,128]{3,2,1,0:T(4,128)(2,1)S(1)} %copy-done.6, f32[16,4,64]{2,1,0:T(4,128)S(1)} %fusion.55, f32[16,4,64,128]{3,2,1,0:T(8,128)} %copy-done.7, pred[16,128]{1,0:T(8,128)(4,1)S(1)} %iota_compare_fusion.4), kind=kOutput, calls=%fused_computation.41 | convolution fusion | flops 137367680 | bytes 5261312 | tf_op jit(solution)/shard_map/ehqk,ekhd->eqhd/dot_general | solution.py:46
  348.7 3.8 convolution_convert_fusion.7
  352.6 0.0 reduce-scatter.6.cloned.1.call-update
  352.6 0.0 all-gather.11.cloned.1.call-start
  352.7 70.8 %reduce-scatter.6.cloned.1.call-done = bf16[1,64,1024]{2,1,0:T(8,128)(2,1)} async-done(((bf16[16,64,1024]{2,1,0:T(8,128)(2,1)}), bf16[1,64,1024]{2,1,0:T(8,128)(2,1)}) %reduce-scatter.6.cloned.1.call-update) | async-done | bytes 131088 | tf_op jit(solution)/shard_map/reduce_scatter | solution.py:57
  423.5 1.1 multiply_reduce_fusion.2
  424.6 1.7 multiply_convert_fusion.2
  426.3 0.0 all-gather.11.cloned.1.call-update
  426.3 0.3 reduce-scatter.8.cloned.1.call-start
  426.6 46.4 %all-gather.11.cloned.1.call-done = bf16[16,64,1024]{2,1,0:T(8,128)(2,1)} async-done(((bf16[1,64,1024]{2,1,0:T(8,128)(2,1)}), bf16[16,64,1024]{2,1,0:T(8,128)(2,1)}) %all-gather.11.cloned.1.call-update) | async-done | bytes 2097168 | tf_op jit(solution)/shard_map/all_gather | solution.py:53
  473.0 14.3 %convolution_convert_fusion.6 = bf16[1024,1024]{1,0:T(8,128)(2,1)} fusion(bf16[2048,1024]{1,0:T(8,128)(2,1)} %param.41, bf16[1024,1024]{1,0:T(8,128)(2,1)} %bitcast.64, bf16[1024,2048]{1,0:T(8,128)(2,1)} %param.40), kind=kOutput, calls=%fused_computation.36 | convolution fusion | flops 8595177472 | bytes 12582912 | tf_op jit(solution)/shard_map/dot_general | solution.py:78
  488.0 69.2 %reduce-scatter.8.cloned.1.call-done = bf16[1,64,1024]{2,1,0:T(8,128)(2,1)} async-done(((bf16[16,64,1024]{2,1,0:T(8,128)(2,1)}), bf16[1,64,1024]{2,1,0:T(8,128)(2,1)}) %reduce-scatter.8.cloned.1.call-update) | async-done | bytes 131088 | tf_op jit(solution)/shard_map/reduce_scatter | solution.py:57
  557.3 1.6 select_convert_fusion
  (51 shorter events, 0.2 us)
Async XLA Ops:
  7.2 94.2 %copy-start = (bf16[512,1024]{1,0:T(8,128)(2,1)S(1)}, bf16[512,1024]{1,0:T(8,128)(2,1)}, u32[]{:S(2)}) copy-start(bf16[512,1024]{1,0:T(8,128)(2,1)} %param.27) | copy-start | bytes 3145732
  7.2 5.0 copy-start.14
  7.2 61.8 %copy-start.16 = (bf16[1024,512]{1,0:T(8,128)(2,1)S(1)}, bf16[1024,512]{1,0:T(8,128)(2,1)}, u32[]{:S(2)}) copy-start(bf16[1024,512]{1,0:T(8,128)(2,1)} %param.25) | copy-start | bytes 3145732
  7.2 61.8 %all-gather.5.cloned.1.call-start = ((), (), s32[]{:S(2)}) async-start(), calls=%async_computation.4 | async-start | bytes 4456448 | tf_op jit(solution)/shard_map/all_gather | solution.py:53
  10.3 173.9 %reduce-scatter.4.cloned.1.call-start = ((), (), s32[]{:S(2)}) async-start(), calls=%async_computation.5 | async-start | bytes 4456448 | tf_op jit(solution)/shard_map/reduce_scatter | solution.py:57
  77.4 6.3 %copy-start.15 = (bf16[16,128,1024]{2,1,0:T(8,128)(2,1)S(1)}, bf16[16,128,1024]{2,1,0:T(8,128)(2,1)}, u32[]{:S(2)}) copy-start(bf16[16,128,1024]{2,1,0:T(8,128)(2,1)} %all-gather.5.cloned.1.call-done) | copy-start | bytes 12582916
  77.4 6.3 %copy-start.17 = (bf16[1024,512]{1,0:T(8,128)(2,1)S(1)}, bf16[1024,512]{1,0:T(8,128)(2,1)}, u32[]{:S(2)}) copy-start(bf16[1024,512]{1,0:T(8,128)(2,1)} %param.26) | copy-start | bytes 3145732
  98.5 1.8 copy-start.5
  105.7 78.6 %copy-start.3 = (bf16[1,128,1024]{2,1,0:T(8,128)(2,1)S(1)}, bf16[1,128,1024]{2,1,0:T(8,128)(2,1)}, u32[]{:S(2)}) copy-start(bf16[1,128,1024]{2,1,0:T(8,128)(2,1)} %param.21) | copy-start | bytes 786436
  105.7 79.7 %copy-start.10 = (f32[1024]{0:T(1024)S(1)}, f32[1024]{0:T(1024)}, u32[]{:S(2)}) copy-start(f32[1024]{0:T(1024)} %param.29) | copy-start | bytes 12292
  105.7 136.1 %all-gather.7.cloned.1.call-start = ((), (), s32[]{:S(2)}) async-start(), calls=%async_computation.6 | async-start | bytes 4456448 | tf_op jit(solution)/shard_map/all_gather | solution.py:53
  187.2 126.1 %all-gather.9.cloned.1.call-start = ((), (), s32[]{:S(2)}) async-start(), calls=%async_computation.7 | async-start | bytes 2228224 | tf_op jit(solution)/shard_map/all_gather | solution.py:53
  246.6 5.5 copy-start.9
  246.6 5.5 copy-start.13
  246.6 71.8 %all-to-all-start = ((bf16[2,8,128,1024]{3,2,0,1:T(8,128)(2,1)}), bf16[2,8,128,1024]{3,2,0,1:T(8,128)(2,1)}, u32[]{:S(2)}, u32[]{:S(2)}) async-start(bf16[2,8,128,1024]{3,2,0,1:T(8,128)(2,1)} %copy.70), calls=%async_computation.1 | async-start | bytes 8388608 | tf_op jit(solution)/shard_map/all_to_all | solution.py:66
  251.3 64.3 %copy-start.11 = (f32[1024]{0:T(1024)S(1)}, f32[1024]{0:T(1024)}, u32[]{:S(2)}) copy-start(f32[1024]{0:T(1024)} %param.34) | copy-start | bytes 12292
  251.3 172.2 %reduce-scatter.6.cloned.1.call-start = ((), (), s32[]{:S(2)}) async-start(), calls=%async_computation.8 | async-start | bytes 2228224 | tf_op jit(solution)/shard_map/reduce_scatter | solution.py:57
  313.2 2.4 copy-start.2
  315.6 1.2 copy-start.18
  318.1 1.2 copy-start.19
  319.3 5.9 %copy-start.20 = (bf16[1024,512]{1,0:T(8,128)(2,1)S(1)}, bf16[1024,512]{1,0:T(8,128)(2,1)}, u32[]{:S(2)}) copy-start(bf16[1024,512]{1,0:T(8,128)(2,1)} %param.37) | copy-start | bytes 3145732
  336.0 1.3 copy-start.7
  337.3 1.6 copy-start.6
  338.9 9.8 %copy-start.21 = (bf16[512,1024]{1,0:T(8,128)(2,1)S(1)}, bf16[512,1024]{1,0:T(8,128)(2,1)}, u32[]{:S(2)}) copy-start(bf16[512,1024]{1,0:T(8,128)(2,1)} %param.38) | copy-start | bytes 3145732
  352.6 71.0 %copy-start.4 = (bf16[1,64,1024]{2,1,0:T(8,128)(2,1)S(1)}, bf16[1,64,1024]{2,1,0:T(8,128)(2,1)}, u32[]{:S(2)}) copy-start(bf16[1,64,1024]{2,1,0:T(8,128)(2,1)} %param.30) | copy-start | bytes 393220
  352.6 72.0 %copy-start.12 = (f32[1024]{0:T(1024)S(1)}, f32[1024]{0:T(1024)}, u32[]{:S(2)}) copy-start(f32[1024]{0:T(1024)} %param.39) | copy-start | bytes 12292
  352.6 120.4 %all-gather.11.cloned.1.call-start = ((), (), s32[]{:S(2)}) async-start(), calls=%async_computation.9 | async-start | bytes 2228224 | tf_op jit(solution)/shard_map/all_gather | solution.py:53
  426.3 131.0 %reduce-scatter.8.cloned.1.call-start = ((), (), s32[]{:S(2)}) async-start(), calls=%async_computation.10 | async-start | bytes 2228224 | tf_op jit(solution)/shard_map/reduce_scatter | solution.py:57
  473.0 85.9 %copy-start.1 = (bf16[512,1024]{1,0:T(8,128)(2,1)S(1)}, bf16[512,1024]{1,0:T(8,128)(2,1)}, u32[]{:S(2)}) copy-start(bf16[512,1024]{1,0:T(8,128)(2,1)} %param.27) | copy-start | bytes 3145732
  487.3 70.0 %copy-start.8 = (bf16[1,64,1024]{2,1,0:T(8,128)(2,1)S(1)}, bf16[1,64,1024]{2,1,0:T(8,128)(2,1)}, u32[]{:S(2)}) copy-start(bf16[1,64,1024]{2,1,0:T(8,128)(2,1)} %reduce-scatter.6.cloned.1.call-done) | copy-start | bytes 393220
Sparse Core Ops, SparseCore 0:
  11.1 57.8 all-gather.4
  105.8 78.3 reduce-scatter.3
  187.6 54.2 all-gather.6
  244.5 68.7 all-gather.8
  352.7 70.7 reduce-scatter.5
  426.4 46.5 all-gather.10
  487.5 69.7 reduce-scatter.7
where the time goes:
time: 567 us; the launch traced here: 566 us
  waiting for transfers between devices  437 us (77%)
  matrix products  67.4 us (12%)
  local copies, waits for them, and re-layouts  24.1 us (4%)
  other arithmetic  16.5 us (3%)
  between operations  15.1 us (3%)
    reduce_scatter x3, waiting for transfers between devices, narrow(): lax.psum_scatter(partial_value.astype(jnp.bfloat16), 'tensor', scatter_di...  219 us
    all_gather x4, waiting for transfers between devices, widen(): return lax.all_gather(values, 'tensor', axis=0, tiled=True)  218 us
    dot_general x6, matrix products, project(): jnp.dot(flat_rows, weight, preferred_element_type=jnp.float32)  27.6 us
    dot_general x3, matrix products, output_terms(): result = jnp.dot(flat_rows, weight, preferred_element_type=jnp.float32)  22.5 us
  transfers between devices with their start and end apart: 8, of which 7 were waited for; matrix products, arithmetic and copies ran while one was open for 2% of the time, Pallas kernels for 0%

commit v1 on v0

--- a/solution.py
+++ b/solution.py
@@ -8,6 +8,11 @@
 NB = 33
 EPSILON = 1e-06
 NEG_FILL = -1e30
+
+
+def swapped_in(shard, axis, d):
+    outgoing = jnp.stack([shard] * lax.axis_size(axis))
+    return jnp.concatenate(lax.all_to_all(outgoing, axis, 0, 0), axis=d)
 
 
 def rms_norm(values, norm_gain):
@@ -50,7 +55,7 @@
 
 
 def widen(values):
-    return lax.all_gather(values, "tensor", axis=0, tiled=True)
+    return swapped_in(values, "tensor", 0)
 
 
 def narrow(partial_value):

time: 567 us -> 593 us (1.046)
  blocking collectives: 0 us -> 89.5 us
  waiting for transfers between devices: 437 us -> 360 us
  starting transfers between devices: 5.45 us -> 17.9 us
    all_gather x4 -> x0, waiting for transfers between devices: 218 us -> none  [widen(): return lax.all_gather(values, 'tensor', axis=0, tiled=True)]
    all_to_all x0 -> x2, blocking collectives: none -> 89.5 us  [swapped_in(): return jnp.concatenate(lax.all_to_all(outgoing, axis, 0, 0), axis=d)]
    all_to_all x0 -> x2, waiting for transfers between devices: none -> 78.7 us  [swapped_in(): return jnp.concatenate(lax.all_to_all(outgoing, axis, 0, 0), axis=d)]
    all_to_all x1, waiting for transfers between devices: 0.01 us -> 54.8 us  [restripe(): lax.all_to_all(shaped, 'dp', split_axis=1, concat_axis=0, tiled=True)]
    all_to_all x0 -> x2, starting transfers between devices: none -> 12 us  [swapped_in(): return jnp.concatenate(lax.all_to_all(outgoing, axis, 0, 0), axis=d)]
    another operation x1 -> x6, local copies, waits for them, and re-layouts: 0.01 us -> 9.66 us  [the longest x4 4.93 us: swapped_in(): outgoing = jnp.stack([shard] * lax.axis_size(axis))]
    reduce_scatter x3, waiting for transfers between devices: 219 us -> 227 us  [narrow(): lax.psum_scatter(partial_value.astype(jnp.bfloat16), 'tensor', scatter_di...]
  transfers between devices with their start and end apart: 8 -> 6, of which waited for: 7 -> 6; matrix products, arithmetic and copies ran while one was open for 2% -> 2% of each run, Pallas kernels for 0% -> 0%
where the time goes in v1:
time: 593 us; the launch traced here: 592 us
  waiting for transfers between devices  360 us (61%)
  blocking collectives  89.5 us (15%)
  matrix products  68.1 us (11%)
  local copies, waits for them, and re-layouts  28.4 us (5%)
  starting transfers between devices  17.9 us (3%)
  between operations  14.7 us (2%)
  other arithmetic  12.6 us (2%)
    reduce_scatter x3, waiting for transfers between devices, narrow(): lax.psum_scatter(partial_value.astype(jnp.bfloat16), 'tensor', scatter_di...  227 us
    all_to_all x2, blocking collectives, swapped_in(): return jnp.concatenate(lax.all_to_all(outgoing, axis, 0, 0), axis=d)  89.5 us
    all_to_all x2, waiting for transfers between devices, swapped_in(): return jnp.concatenate(lax.all_to_all(outgoing, axis, 0, 0), axis=d)  78.7 us
    all_to_all x1, waiting for transfers between devices, restripe(): lax.all_to_all(shaped, 'dp', split_axis=1, concat_axis=0, tiled=True)  54.8 us
    dot_general x6, matrix products, project(): jnp.dot(flat_rows, weight, preferred_element_type=jnp.float32)  29.7 us
    dot_general x3, matrix products, output_terms(): result = jnp.dot(flat_rows, weight, preferred_element_type=jnp.float32)  21.8 us
    all_to_all x2, starting transfers between devices, swapped_in(): return jnp.concatenate(lax.all_to_all(outgoing, axis, 0, 0), axis=d)  12 us
  transfers between devices with their start and end apart: 6, of which 6 were waited for; matrix products, arithmetic and copies ran while one was open for 2% of the time, Pallas kernels for 0%

profile of v1, /device:TPU:0, one launch (start us, length us, event | category | flops | bytes accessed | tf_op | source)
XLA Modules:
  0.0 591.6 jit_solution(14725179668424665748)
XLA Ops:
  7.2 1.2 fusion.44
  8.4 1.1 fusion.47
  9.5 2.5 stack.8
  12.0 8.3 %all-to-all-start = ((bf16[16,1,128,1024]{3,2,1,0:T(8,128)(2,1)}), bf16[16,1,128,1024]{3,2,1,0:T(8,128)(2,1)}, u32[]{:S(2)}, u32[]{:S(2)}) async-start(bf16[16,1,128,1024]{3,2,1,0:T(8,128)(2,1)} %stack.8), calls=%async_computation | async-start | bytes 8388608 | tf_op jit(solution)/shard_map/all_to_all | solution.py:15
  20.3 0.0 reduce-scatter.4.cloned.1.call-start
  20.4 1.0 fusion.34
  21.4 0.1 copy.77
  21.5 0.1 dynamic_slice.8
  21.6 0.1 iota_compare_fusion.6
  21.7 54.1 %all-to-all-done = bf16[16,1,128,1024]{3,2,1,0:T(8,128)(2,1)} async-done(((bf16[16,1,128,1024]{3,2,1,0:T(8,128)(2,1)}), bf16[16,1,128,1024]{3,2,1,0:T(8,128)(2,1)}, u32[]{:S(2)}, u32[]{:S(2)}) %all-to-all-start) | async-done | bytes 4194336 | tf_op jit(solution)/shard_map/all_to_all | solution.py:15
  75.8 5.9 convolution_convert_fusion.2
  81.7 2.5 reshape_reshape.38
  84.2 6.2 %convolution_convert_fusion.3 = bf16[2048,512]{1,0:T(8,128)(2,1)} fusion(bf16[2048,1024]{1,0:T(8,128)(2,1)} %bitcast.1, bf16[1024,512]{1,0:T(8,128)(2,1)} %param.24), kind=kOutput, calls=%fused_computation.16 | convolution fusion | flops 2148532224 | bytes 7340032 | tf_op jit(solution)/shard_map/dot_general | solution.py:77
  90.5 5.9 convolution_convert_fusion.4
  96.4 4.0 reshape_reshape.36
  100.3 4.0 reshape_reshape.37
  104.3 3.2 fusion.15
  107.5 1.8 fusion.61
  109.2 0.9 fusion.23
  110.1 4.3 convolution_convert_fusion.5
  114.5 87.8 %reduce-scatter.4.cloned.1.call-done = bf16[1,128,1024]{2,1,0:T(8,128)(2,1)} async-done(((bf16[16,128,1024]{2,1,0:T(8,128)(2,1)}), bf16[1,128,1024]{2,1,0:T(8,128)(2,1)}) %reduce-scatter.4.cloned.1.call-update) | async-done | bytes 262160 | tf_op jit(solution)/shard_map/reduce_scatter | solution.py:62
  202.3 1.1 multiply_reduce_fusion
  203.5 1.1 multiply_convert_fusion
  204.5 0.5 stack.9
  205.1 0.2 copy-done.8
  205.2 55.8 %all_to_all.35 = bf16[16,1,128,1024]{3,2,1,0:T(8,128)(2,1)} all-to-all(bf16[16,1,128,1024]{3,2,1,0:T(8,128)(2,1)S(1)} %stack.9), channel_id=1, replica_groups=mesh['dp'=8,'tensor'=16] {'tensor'}, dimensions={0} | all-to-all | bytes 8388608 | tf_op jit(solution)/shard_map/all_to_all | solution.py:15
  261.1 1.7 stack.10
  262.7 3.7 all-to-all-start.3
  266.5 4.7 copy.81
  271.2 24.5 %all-to-all-done.3 = bf16[16,1,64,1024]{3,2,1,0:T(8,128)(2,1)S(1)} async-done(((bf16[16,1,64,1024]{3,2,1,0:T(8,128)(2,1)}), bf16[16,1,64,1024]{3,2,1,0:T(8,128)(2,1)S(1)}, u32[]{:S(2)}, u32[]{:S(2)}) %all-to-all-start.3) | async-done | bytes 2097184 | tf_op jit(solution)/shard_map/all_to_all | solution.py:15
  295.7 5.5 all-to-all-start.2
  301.2 0.3 reduce-scatter.6.cloned.1.call-start
  301.5 0.1 reshape.183
  301.6 0.3 dynamic-slice_reduce_fusion
  301.9 0.1 lt.72
  302.0 0.1 iota_compare_fusion.4
  302.1 0.2 fusion.49
  302.2 0.6 fusion.3
  302.9 0.1 rsqrt.38
  302.9 0.6 fusion.6
  303.6 0.6 copy-done.17
  304.2 1.2 convolution_convert_fusion.8
  305.4 0.3 reshape_reshape.42
  305.7 54.8 %all-to-all-done.2 = bf16[2,8,128,1024]{3,2,0,1:T(8,128)(2,1)} async-done(((bf16[2,8,128,1024]{3,2,0,1:T(8,128)(2,1)}), bf16[2,8,128,1024]{3,2,0,1:T(8,128)(2,1)}, u32[]{:S(2)}, u32[]{:S(2)}) %all-to-all-start.2) | async-done | bytes 4194336 | tf_op jit(solution)/shard_map/all_to_all | solution.py:71
  360.6 5.9 convolution_convert_fusion
  366.5 4.5 convolution_convert_fusion.1
  371.0 2.1 reshape_reshape.41
  373.1 2.5 reshape_reshape.43
  375.7 1.5 fusion.12
  377.2 1.3 copy-done.6
  378.5 1.2 fusion.62
  379.7 0.4 copy-done.5
  380.1 9.9 %fusion.30 = bf16[16,4,8,8,128]{4,3,2,1,0:T(8,128)(2,1)} fusion(bf16[16,128,4,128]{3,2,1,0:T(4,128)(2,1)S(1)} %copy-done.5, f32[16,4,64]{2,1,0:T(4,128)S(1)} %fusion.62, f32[16,4,64,128]{3,2,1,0:T(8,128)} %copy-done.6, pred[16,128]{1,0:T(8,128)(4,1)S(1)} %iota_compare_fusion.4), kind=kOutput, calls=%fused_computation.45 | convolution fusion | flops 137367680 | bytes 5261312 | tf_op jit(solution)/shard_map/ehqk,ekhd->eqhd/dot_general | solution.py:51
  390.0 3.8 convolution_convert_fusion.7
  393.8 0.0 reduce-scatter.6.cloned.1.call-update
  393.8 0.0 reduce-scatter.8.cloned.1.call-start
  393.9 71.4 %reduce-scatter.6.cloned.1.call-done = bf16[1,64,1024]{2,1,0:T(8,128)(2,1)} async-done(((bf16[16,64,1024]{2,1,0:T(8,128)(2,1)}), bf16[1,64,1024]{2,1,0:T(8,128)(2,1)}) %reduce-scatter.6.cloned.1.call-update) | async-done | bytes 131088 | tf_op jit(solution)/shard_map/reduce_scatter | solution.py:62
  465.2 1.1 multiply_reduce_fusion.1
  466.3 1.0 fusion.48
  467.3 0.3 stack.11
  467.6 33.7 %all_to_all.36 = bf16[16,1,64,1024]{3,2,1,0:T(8,128)(2,1)S(1)} all-to-all(bf16[16,1,64,1024]{3,2,1,0:T(8,128)(2,1)S(1)} %stack.11), channel_id=1, replica_groups=mesh['dp'=8,'tensor'=16] {'tensor'}, dimensions={0} | all-to-all | bytes 4194304 | tf_op jit(solution)/shard_map/all_to_all | solution.py:15
  501.3 13.7 %convolution_convert_fusion.6 = bf16[1024,1024]{1,0:T(8,128)(2,1)} fusion(bf16[2048,1024]{1,0:T(8,128)(2,1)} %param.41, bf16[1024,1024]{1,0:T(8,128)(2,1)S(1)} %bitcast.78, bf16[1024,2048]{1,0:T(8,128)(2,1)} %param.40), kind=kOutput, calls=%fused_computation.40 | convolution fusion | flops 8595177472 | bytes 12582912 | tf_op jit(solution)/shard_map/dot_general | solution.py:83
  515.7 67.7 %reduce-scatter.8.cloned.1.call-done = bf16[1,64,1024]{2,1,0:T(8,128)(2,1)} async-done(((bf16[16,64,1024]{2,1,0:T(8,128)(2,1)}), bf16[1,64,1024]{2,1,0:T(8,128)(2,1)}) %reduce-scatter.8.cloned.1.call-update) | async-done | bytes 131088 | tf_op jit(solution)/shard_map/reduce_scatter | solution.py:62
  583.4 1.6 select_convert_fusion
  (50 shorter events, 0.2 us)
Async XLA Ops:
  7.2 103.0 %copy-start = (bf16[512,1024]{1,0:T(8,128)(2,1)S(1)}, bf16[512,1024]{1,0:T(8,128)(2,1)}, u32[]{:S(2)}) copy-start(bf16[512,1024]{1,0:T(8,128)(2,1)} %param.27) | copy-start | bytes 3145732
  12.0 8.4 %copy-start.21 = (f32[4,33]{1,0:T(4,128)S(1)}, f32[4,33]{1,0:T(4,128)}, u32[]{:S(2)}) copy-start(f32[4,33]{1,0:T(4,128)} %param.28) | copy-start | bytes 1588
  12.0 9.6 %copy-start.14 = (s32[128]{0:T(128)S(1)}, s32[128]{0:T(128)}, u32[]{:S(2)}) copy-start(s32[128]{0:T(128)} %param.22) | copy-start | bytes 1540
  12.0 63.8 %copy-start.15 = (bf16[1024,512]{1,0:T(8,128)(2,1)S(1)}, bf16[1024,512]{1,0:T(8,128)(2,1)}, u32[]{:S(2)}) copy-start(bf16[1024,512]{1,0:T(8,128)(2,1)} %param.25) | copy-start | bytes 3145732
  12.0 63.8 %all-to-all-start = ((bf16[16,1,128,1024]{3,2,1,0:T(8,128)(2,1)}), bf16[16,1,128,1024]{3,2,1,0:T(8,128)(2,1)}, u32[]{:S(2)}, u32[]{:S(2)}) async-start(bf16[16,1,128,1024]{3,2,1,0:T(8,128)(2,1)} %stack.8), calls=%async_computation | async-start | bytes 8388608 | tf_op jit(solution)/shard_map/all_to_all | solution.py:15
  20.3 182.0 %reduce-scatter.4.cloned.1.call-start = ((), (), s32[]{:S(2)}) async-start(), calls=%async_computation.8 | async-start | bytes 4456448 | tf_op jit(solution)/shard_map/reduce_scatter | solution.py:62
  84.2 6.3 %copy-start.16 = (bf16[1024,512]{1,0:T(8,128)(2,1)S(1)}, bf16[1024,512]{1,0:T(8,128)(2,1)}, u32[]{:S(2)}) copy-start(bf16[1024,512]{1,0:T(8,128)(2,1)} %param.26) | copy-start | bytes 3145732
  107.5 1.8 copy-start.4
  114.5 87.9 %copy-start.2 = (bf16[1,128,1024]{2,1,0:T(8,128)(2,1)S(1)}, bf16[1,128,1024]{2,1,0:T(8,128)(2,1)}, u32[]{:S(2)}) copy-start(bf16[1,128,1024]{2,1,0:T(8,128)(2,1)} %param.21) | copy-start | bytes 786436
  114.5 89.0 %copy-start.10 = (f32[1024]{0:T(1024)S(1)}, f32[1024]{0:T(1024)}, u32[]{:S(2)}) copy-start(f32[1024]{0:T(1024)} %param.29) | copy-start | bytes 12292
  204.5 0.7 copy-start.8
  205.2 55.8 %copy-start.3 = (bf16[1,64,1024]{2,1,0:T(8,128)(2,1)S(1)}, bf16[1,64,1024]{2,1,0:T(8,128)(2,1)}, u32[]{:S(2)}) copy-start(bf16[1,64,1024]{2,1,0:T(8,128)(2,1)} %param.30) | copy-start | bytes 393220
  262.7 33.0 %all-to-all-start.3 = ((bf16[16,1,64,1024]{3,2,1,0:T(8,128)(2,1)}), bf16[16,1,64,1024]{3,2,1,0:T(8,128)(2,1)S(1)}, u32[]{:S(2)}, u32[]{:S(2)}) async-start(bf16[16,1,64,1024]{3,2,1,0:T(8,128)(2,1)} %stack.10), calls=%async_computation.4 | async-start | bytes 4194304 | tf_op jit(solution)/shard_map/all_to_all | solution.py:15
  271.2 30.9 %copy-start.9 = (bf16[8,1024]{1,0:T(8,128)(2,1)S(1)}, bf16[8,1024]{1,0:T(8,128)(2,1)}, u32[]{:S(2)}) copy-start(bf16[8,1024]{1,0:T(8,128)(2,1)} %param.33) | copy-start | bytes 49156
  271.2 30.9 %copy-start.13 = (s32[16]{0:T(128)S(1)}, s32[16]{0:T(128)}, u32[]{:S(2)}) copy-start(s32[16]{0:T(128)} %param.32) | copy-start | bytes 196
  295.7 64.8 %all-to-all-start.2 = ((bf16[2,8,128,1024]{3,2,0,1:T(8,128)(2,1)}), bf16[2,8,128,1024]{3,2,0,1:T(8,128)(2,1)}, u32[]{:S(2)}, u32[]{:S(2)}) async-start(bf16[2,8,128,1024]{3,2,0,1:T(8,128)(2,1)} %copy.81), calls=%async_computation.3 | async-start | bytes 8388608 | tf_op jit(solution)/shard_map/all_to_all | solution.py:71
  301.2 1.7 copy-start.12
  301.2 164.0 %reduce-scatter.6.cloned.1.call-start = ((), (), s32[]{:S(2)}) async-start(), calls=%async_computation.9 | async-start | bytes 2228224 | tf_op jit(solution)/shard_map/reduce_scatter | solution.py:62
  302.9 1.2 copy-start.17
  305.4 55.1 %copy-start.18 = (bf16[1024,512]{1,0:T(8,128)(2,1)S(1)}, bf16[1024,512]{1,0:T(8,128)(2,1)}, u32[]{:S(2)}) copy-start(bf16[1024,512]{1,0:T(8,128)(2,1)} %param.36) | copy-start | bytes 3145732
  360.6 5.9 %copy-start.19 = (bf16[1024,512]{1,0:T(8,128)(2,1)S(1)}, bf16[1024,512]{1,0:T(8,128)(2,1)}, u32[]{:S(2)}) copy-start(bf16[1024,512]{1,0:T(8,128)(2,1)} %param.37) | copy-start | bytes 3145732
  377.2 1.3 copy-start.6
  378.5 1.6 copy-start.5
  380.1 9.9 %copy-start.20 = (bf16[512,1024]{1,0:T(8,128)(2,1)S(1)}, bf16[512,1024]{1,0:T(8,128)(2,1)}, u32[]{:S(2)}) copy-start(bf16[512,1024]{1,0:T(8,128)(2,1)} %param.38) | copy-start | bytes 3145732
  393.8 72.5 %copy-start.11 = (f32[1024]{0:T(1024)S(1)}, f32[1024]{0:T(1024)}, u32[]{:S(2)}) copy-start(f32[1024]{0:T(1024)} %param.39) | copy-start | bytes 12292
  393.8 189.6 %reduce-scatter.8.cloned.1.call-start = ((), (), s32[]{:S(2)}) async-start(), calls=%async_computation.10 | async-start | bytes 2228224 | tf_op jit(solution)/shard_map/reduce_scatter | solution.py:62
  501.3 83.8 %copy-start.1 = (bf16[512,1024]{1,0:T(8,128)(2,1)S(1)}, bf16[512,1024]{1,0:T(8,128)(2,1)}, u32[]{:S(2)}) copy-start(bf16[512,1024]{1,0:T(8,128)(2,1)} %param.27) | copy-start | bytes 3145732
  515.0 68.4 %copy-start.7 = (bf16[1,64,1024]{2,1,0:T(8,128)(2,1)S(1)}, bf16[1,64,1024]{2,1,0:T(8,128)(2,1)}, u32[]{:S(2)}) copy-start(bf16[1,64,1024]{2,1,0:T(8,128)(2,1)} %reduce-scatter.6.cloned.1.call-done) | copy-start | bytes 393220
Sparse Core Ops, SparseCore 0:
  114.6 87.6 reduce-scatter.3
  393.9 71.2 reduce-scatter.5
  515.1 68.2 reduce-scatter.7
